TPU v7x, 32 devices: a whole 2x2x4 slice. The times are simulated.
32 devices in a mesh: pairs: 32 (over z, y, x, core).
Axes of the slice: x: 2, y: 2, z: 4, core: 2. Of those that a mesh axis runs over, the one named last changes fastest.
Arguments:
- pno_basis: bfloat16 [256, 192, 128], P('pairs'), may hold values from -0.4375 to 0.4375
- pno_count: int32 [256], P('pairs'), may hold values from 64 to 128
- partner_owner: int32 [256, 12], P('pairs'), may hold values from 0 to 31, all different within a row; in each aligned block of 8 rows (0 to 7, 8 to 15, ...) at most 3 rows name the same one
- partner_local: int32 [256, 12], P('pairs'), may hold values from 0 to 7
- exchange_k: bfloat16 [256, 128, 128], P('pairs'), may hold values from -6 to 6
- ladder_factor: bfloat16 [256, 40, 128, 128], P('pairs'), may hold values from -0.15625 to 0.15625
- pno_energy: float32 [256, 128], P('pairs'), may hold values from 0.3 to 3
- occ_energy: float32 [256], P('pairs'), may hold values from -2 to -0.6
- coupling_fock: bfloat16 [256, 12], P('pairs'), may hold values from -3 to 3
Outputs:
- amplitudes: float32 [256, 128, 128], P('pairs')
Inputs may be any that keep to these rules, and one draw needn't show every extreme that they name: `partner_owner`: the 12 partners of one pair have different owners. Among the 8 pairs of one device no device is named more than 3 times, and in some devices' pairs one device is named exactly 3 times. Partner c of pair p is the pair numbered partner_owner[p, c] * 8 + partner_local[p, c]. Pair p uses its first pno_count[p] orbitals; the others are padding.
All inputs are finite; a program needn't handle non-finite values.
Results may differ from a plain program's by a relative error of at most 0.009.
Values may be sent and summed in bfloat16 or wider, within the bound.
A program may use at most 128 MiB of HBM per device.

v0:
```python
import jax
import jax.numpy as jnp
from jax import lax
from jax.sharding import PartitionSpec as P

ITERS = 3


level_shift = 0.3


def gather_rows(source_rows, chosen, usable):
    picked = source_rows[jnp.clip(chosen, 0, source_rows.shape[0] - 1)]
    extended = usable.reshape(usable.shape + (1,) * (picked.ndim - usable.ndim))
    return jnp.where(extended, picked, jnp.zeros_like(picked))


def shards(
    pno_basis,
    pno_count,
    partner_owner,
    partner_local,
    exchange_k,
    ladder_factor,
    pno_energy,
    occ_energy,
    coupling_fock,
):
    peer_count = lax.axis_size("pairs")
    own_pairs, domain, orbitals = pno_basis.shape
    fitted = ladder_factor.shape[1]
    partners = partner_owner.shape[1]
    listed = own_pairs * partners
    slot_count = max(2, (listed + peer_count - 1) // peer_count)
    columns = lax.broadcasted_iota(jnp.int32, (own_pairs, orbitals), 1)
    live_cols = (columns < pno_count[:, None]).astype(jnp.float32)
    masked_basis = pno_basis * live_cols[:, None, :].astype(jnp.bfloat16)
    flat_owner = partner_owner.reshape(listed)
    flat_local = partner_local.reshape(listed)
    owner_onehot = (
        flat_owner[:, None] == lax.broadcasted_iota(jnp.int32, (listed, peer_count), 1)
    ).astype(jnp.int32)
    before = jnp.cumsum(owner_onehot, axis=0) - owner_onehot
    slot_rank = jnp.sum(before * owner_onehot, axis=1)
    flat_slot = flat_owner * slot_count + slot_rank
    slot_onehot = (
        slot_rank[:, None] == lax.broadcasted_iota(jnp.int32, (listed, slot_count), 1)
    ).astype(jnp.int32)
    labelled = slot_onehot * (flat_local + 1)[:, None]
    wanted = jnp.sum(owner_onehot[:, :, None] * labelled[:, None, :], axis=0) - 1
    asked_rows = lax.all_to_all(wanted, "pairs", split_axis=0, concat_axis=0, tiled=True)
    asked_usable = asked_rows >= 0
    sent_basis = gather_rows(masked_basis, asked_rows, asked_usable)
    arrived_basis = lax.all_to_all(sent_basis, "pairs", split_axis=0, concat_axis=0, tiled=True)
    partner_basis = arrived_basis.reshape(peer_count * slot_count, domain, orbitals)[flat_slot]
    partner_basis = partner_basis.reshape(own_pairs, partners, domain, orbitals)
    margin = jnp.einsum(
        "rva,rcvb->rcab", masked_basis, partner_basis, preferred_element_type=jnp.float32
    ).astype(jnp.bfloat16)
    energy_sum = pno_energy[:, :, None] + pno_energy[:, None, :] - occ_energy[:, None, None]
    divisor = energy_sum + level_shift
    driving = exchange_k.astype(jnp.float32) * (live_cols[:, :, None] * live_cols[:, None, :])
    amplitudes = -driving / divisor
    weights = coupling_fock.astype(jnp.float32)
    group_width = 8
    for iteration in range(ITERS):
        sent_amps = amplitudes.astype(jnp.bfloat16)
        sent_rows = gather_rows(sent_amps, asked_rows, asked_usable)
        arrived_amps = lax.all_to_all(sent_rows, "pairs", split_axis=0, concat_axis=0, tiled=True)

        def add_group(group_index, total):
            factors = lax.dynamic_slice_in_dim(
                ladder_factor, group_index * group_width, group_width, 1
            )
            ladder_half = jnp.einsum(
                "rqac,rcd->rqad", factors, sent_amps, preferred_element_type=jnp.float32
            ).astype(jnp.bfloat16)
            return total + jnp.einsum(
                "rqad,rqbd->rab", ladder_half, factors, preferred_element_type=jnp.float32
            )

        ladder = lax.fori_loop(
            0,
            fitted // group_width,
            add_group,
            jnp.zeros((own_pairs, orbitals, orbitals), jnp.float32),
        )
        partner_amps = arrived_amps.reshape(peer_count * slot_count, orbitals, orbitals)[flat_slot]
        partner_amps = partner_amps.reshape(own_pairs, partners, orbitals, orbitals)
        left_half = jnp.einsum(
            "rcab,rcbd->rcad", margin, partner_amps, preferred_element_type=jnp.float32
        )
        left_half = (left_half * weights[:, :, None, None]).astype(jnp.bfloat16)
        gathered_terms = jnp.einsum(
            "rcad,rced->rcae", left_half, margin, preferred_element_type=jnp.float32
        ).astype(jnp.bfloat16)
        coupled = jnp.sum(gathered_terms, axis=1, dtype=jnp.float32)
        residual = driving + energy_sum * amplitudes + coupled + ladder
        amplitudes = amplitudes - residual / divisor
    return amplitudes


def solution(mesh):
    return jax.shard_map(
        shards,
        mesh=mesh,
        in_specs=(
            P("pairs", None, None),
            P("pairs"),
            P("pairs", None),
            P("pairs", None),
            P("pairs", None, None),
            P("pairs", None, None, None),
            P("pairs", None),
            P("pairs"),
            P("pairs", None),
        ),
        out_specs=P("pairs", None, None),
        check_vma=False,
    )
```

profile of v0, /device:TPU:0, one launch (start us, length us, event | category | flops | bytes accessed | tf_op | source)
XLA Modules:
  0.0 400.8 jit_solution(16633422981414817861)
XLA Ops:
  2.9 7.3 %all-to-all-start = ((s32[32,1,3]{2,1,0:T(1,128)}), s32[32,1,3]{2,1,0:T(1,128)S(1)}, u32[]{:S(2)}, u32[]{:S(2)}) async-start(s32[32,1,3]{2,1,0:T(1,128)} %copy.46), calls=%async_computation | async-start | bytes 32768 | tf_op jit(solution)/shard_map/all_to_all | solution.py:51
  12.3 5.0 %all-to-all-done = s32[32,1,3]{2,1,0:T(1,128)S(1)} async-done(((s32[32,1,3]{2,1,0:T(1,128)}), s32[32,1,3]{2,1,0:T(1,128)S(1)}, u32[]{:S(2)}, u32[]{:S(2)}) %all-to-all-start) | async-done | bytes 416 | tf_op jit(solution)/shard_map/all_to_all | solution.py:51
  28.0 4.9 %broadcast_select_fusion = bf16[32,3,192,128]{3,2,1,0:T(8,128)(2,1)} fusion(bf16[32,3,192,128]{3,2,1,0:T(8,128)(2,1)} %bitcast.85, pred[32,3]{1,0:T(8,128)(4,1)S(1)} %bitcast.96), kind=kLoop, calls=%fused_computation.38 | loop fusion | flops 2359296 | bytes 9437280 | tf_op jit(solution)/shard_map/jit(_where)/select_n | solution.py:15
  32.9 63.0 %all-to-all-done.2 = bf16[32,3,128,128]{3,2,1,0:T(8,128)(2,1)} async-done(((bf16[32,3,128,128]{3,2,1,0:T(8,128)(2,1)}), bf16[32,3,128,128]{3,2,1,0:T(8,128)(2,1)}, u32[]{:S(2)}, u32[]{:S(2)}) %all-to-all-start.2) | async-done | bytes 3145760 | tf_op jit(solution)/shard_map/all_to_all | solution.py:69
  100.2 18.3 %while.42 = (s32[]{:T(128)}, f32[8,128,128]{2,1,0:T(8,128)S(1)}, bf16[8,40,128,128]{3,2,1,0:T(8,128)(2,1)}, bf16[8,128,128]{2,1,0:T(8,128)(2,1)S(1)}, s32[]{:T(128)}, /*index=5*/s32[]{:T(128)}, s32[]{:T(128)}, s32[]{:T(128)}) while((s32[]{:T(128)}, f32[8,128,128]{2,1,0:T(8,128)S(1)}, bf16[8,40,128,128]{3,2,1,0:T(8,128)(2,1)}, ...), condition=%wide.region_5.6_spmd.clone, body=%wide.region_4.5_spmd.clone.sunk | while | flops 538181632 | bytes 5506700 | solution.py:82
  118.6 4.6 %gather_fusion.3 = bf16[96,128,128]{2,1,0:T(8,128)(2,1)} fusion(bf16[96,128,128]{2,1,0:T(8,128)(2,1)} %bitcast.10, s32[1024]{0:T(1024)S(1)} %pad_clamp_fusion), kind=kCustom, calls=%fused_computation.3 | custom fusion | bytes 6291840 | tf_op jit(solution)/shard_map/gather | solution.py:88
  123.2 81.9 %all-to-all-done.1 = bf16[32,3,192,128]{3,2,1,0:T(8,128)(2,1)} async-done(((bf16[32,3,192,128]{3,2,1,0:T(8,128)(2,1)}), bf16[32,3,192,128]{3,2,1,0:T(8,128)(2,1)}, u32[]{:S(2)}, u32[]{:S(2)}) %all-to-all-start.1) | async-done | bytes 4718624 | tf_op jit(solution)/shard_map/all_to_all | solution.py:54
  205.1 5.8 %gather_fusion.1 = bf16[96,192,128]{2,1,0:T(8,128)(2,1)} fusion(bf16[96,192,128]{2,1,0:T(8,128)(2,1)} %bitcast.3, s32[1024]{0:T(1024)S(1)} %pad_clamp_fusion), kind=kCustom, calls=%fused_computation.1 | custom fusion | bytes 9437568 | tf_op jit(solution)/shard_map/gather | solution.py:55
  210.9 6.1 %convolution_convert_fusion = bf16[8,12,128,128]{3,2,1,0:T(8,128)(2,1)} fusion(bf16[8,12,192,128]{3,2,1,0:T(8,128)(2,1)} %bitcast.86, bf16[8,192,128]{2,1,0:T(8,128)(2,1)S(1)} %broadcast_multiply_fusion), kind=kOutput, calls=%fused_computation.51 | convolution fusion | flops 605552640 | bytes 8257536 | tf_op jit(solution)/shard_map/rva,rcvb->rcab/dot_general | solution.py:57
  217.0 6.0 %convert_reduce_fusion.2 = f32[8,128,128]{2,1,0:T(8,128)S(1)} fusion(bf16[8,12,128,128]{3,2,1,0:T(8,128)(2,1)} %convolution_convert_fusion, f32[8,12]{1,0:T(8,128)S(1)} %convert_element_type.103, bf16[8,12,128,128]{3,2,1,0:T(8,128)(2,1)} %bitcast.92), kind=kOutput, calls=%fused_computation.36 | convolution fusion | flops 813039616 | bytes 6816128 | tf_op jit(solution)/shard_map/rcad,rced->rcae/dot_general | solution.py:94
  231.4 21.9 %while.43 = (s32[]{:T(128)}, f32[8,128,128]{2,1,0:T(8,128)}, bf16[8,40,128,128]{3,2,1,0:T(8,128)(2,1)}, bf16[8,128,128]{2,1,0:T(8,128)(2,1)S(1)}, s32[]{:T(128)}, /*index=5*/s32[]{:T(128)}, s32[]{:T(128)}, s32[]{:T(128)}) while((s32[]{:T(128)}, f32[8,128,128]{2,1,0:T(8,128)}, bf16[8,40,128,128]{3,2,1,0:T(8,128)(2,1)}, ...), condition=%wide.region_8.9_spmd.clone, body=%wide.region_7.8_spmd.clone.sunk | while | flops 538181632 | bytes 5506700 | solution.py:82
  235.7 4.4 %fusion.129 = f32[8,128,128]{2,1,0:T(8,128)} fusion(bf16[8,40,128,128]{3,2,1,0:T(8,128)(2,1)} %get-tuple-element.437, s32[]{:T(128)S(6)} %select_n.82, f32[8,128,128]{2,1,0:T(8,128)} %get-tuple-element.428, bf16[8,128,128]{2,1,0:T(8,128)(2,1)S(1)} %get-tuple-element.438, pred[]{:T(512)S(6)} %compare.10), kind=kOutput, calls=%fused_computation.21.clone.1 | convolution fusion | flops 538181632 | bytes 5506560 | tf_op jit(solution)/shard_map/while/body/eval_jaxpr/rqad,rqbd->rab/dot_general | solution.py:78
  240.1 4.4 %fusion.129 = f32[8,128,128]{2,1,0:T(8,128)} fusion(bf16[8,40,128,128]{3,2,1,0:T(8,128)(2,1)} %get-tuple-element.437, s32[]{:T(128)S(6)} %select_n.82, f32[8,128,128]{2,1,0:T(8,128)} %get-tuple-element.428, bf16[8,128,128]{2,1,0:T(8,128)(2,1)S(1)} %get-tuple-element.438, pred[]{:T(512)S(6)} %compare.10), kind=kOutput, calls=%fused_computation.21.clone.1 | convolution fusion | flops 538181632 | bytes 5506560 | tf_op jit(solution)/shard_map/while/body/eval_jaxpr/rqad,rqbd->rab/dot_general | solution.py:78
  244.5 4.4 %fusion.129 = f32[8,128,128]{2,1,0:T(8,128)} fusion(bf16[8,40,128,128]{3,2,1,0:T(8,128)(2,1)} %get-tuple-element.437, s32[]{:T(128)S(6)} %select_n.82, f32[8,128,128]{2,1,0:T(8,128)} %get-tuple-element.428, bf16[8,128,128]{2,1,0:T(8,128)(2,1)S(1)} %get-tuple-element.438, pred[]{:T(512)S(6)} %compare.10), kind=kOutput, calls=%fused_computation.21.clone.1 | convolution fusion | flops 538181632 | bytes 5506560 | tf_op jit(solution)/shard_map/while/body/eval_jaxpr/rqad,rqbd->rab/dot_general | solution.py:78
  248.9 4.4 %fusion.129 = f32[8,128,128]{2,1,0:T(8,128)} fusion(bf16[8,40,128,128]{3,2,1,0:T(8,128)(2,1)} %get-tuple-element.437, s32[]{:T(128)S(6)} %select_n.82, f32[8,128,128]{2,1,0:T(8,128)} %get-tuple-element.428, bf16[8,128,128]{2,1,0:T(8,128)(2,1)S(1)} %get-tuple-element.438, pred[]{:T(512)S(6)} %compare.10), kind=kOutput, calls=%fused_computation.21.clone.1 | convolution fusion | flops 538181632 | bytes 5506560 | tf_op jit(solution)/shard_map/while/body/eval_jaxpr/rqad,rqbd->rab/dot_general | solution.py:78
  253.2 49.4 %all-to-all-done.3 = bf16[32,3,128,128]{3,2,1,0:T(8,128)(2,1)S(1)} async-done(((bf16[32,3,128,128]{3,2,1,0:T(8,128)(2,1)}), bf16[32,3,128,128]{3,2,1,0:T(8,128)(2,1)S(1)}, u32[]{:S(2)}, u32[]{:S(2)}) %all-to-all-start.3) | async-done | bytes 3145760 | tf_op jit(solution)/shard_map/all_to_all | solution.py:69
  305.3 6.0 %convert_reduce_fusion.1 = f32[8,128,128]{2,1,0:T(8,128)S(1)} fusion(bf16[8,12,128,128]{3,2,1,0:T(8,128)(2,1)} %convolution_convert_fusion, f32[8,12]{1,0:T(8,128)S(1)} %convert_element_type.103, bf16[8,12,128,128]{3,2,1,0:T(8,128)(2,1)} %bitcast.94), kind=kOutput, calls=%fused_computation.34 | convolution fusion | flops 813039616 | bytes 6816128 | tf_op jit(solution)/shard_map/rcad,rced->rcae/dot_general | solution.py:94
  319.5 21.9 %while.44 = (s32[]{:T(128)}, f32[8,128,128]{2,1,0:T(8,128)}, bf16[8,40,128,128]{3,2,1,0:T(8,128)(2,1)}, bf16[8,128,128]{2,1,0:T(8,128)(2,1)S(1)}, s32[]{:T(128)}, /*index=5*/s32[]{:T(128)}, s32[]{:T(128)}, s32[]{:T(128)}) while((s32[]{:T(128)}, f32[8,128,128]{2,1,0:T(8,128)}, bf16[8,40,128,128]{3,2,1,0:T(8,128)(2,1)}, ...), condition=%wide.region_11.12_spmd.clone, body=%wide.region_10.11_spmd.clone.sunk | while | flops 538181632 | bytes 5506700 | solution.py:82
  323.9 4.4 %fusion.134 = f32[8,128,128]{2,1,0:T(8,128)} fusion(bf16[8,40,128,128]{3,2,1,0:T(8,128)(2,1)} %get-tuple-element.461, s32[]{:T(128)S(6)} %select_n.83, f32[8,128,128]{2,1,0:T(8,128)} %get-tuple-element.452, bf16[8,128,128]{2,1,0:T(8,128)(2,1)S(1)} %get-tuple-element.462, pred[]{:T(512)S(6)} %compare.11), kind=kOutput, calls=%fused_computation.29.clone.1 | convolution fusion | flops 538181632 | bytes 5506560 | tf_op jit(solution)/shard_map/while/body/eval_jaxpr/rqad,rqbd->rab/dot_general | solution.py:78
  328.2 4.4 %fusion.134 = f32[8,128,128]{2,1,0:T(8,128)} fusion(bf16[8,40,128,128]{3,2,1,0:T(8,128)(2,1)} %get-tuple-element.461, s32[]{:T(128)S(6)} %select_n.83, f32[8,128,128]{2,1,0:T(8,128)} %get-tuple-element.452, bf16[8,128,128]{2,1,0:T(8,128)(2,1)S(1)} %get-tuple-element.462, pred[]{:T(512)S(6)} %compare.11), kind=kOutput, calls=%fused_computation.29.clone.1 | convolution fusion | flops 538181632 | bytes 5506560 | tf_op jit(solution)/shard_map/while/body/eval_jaxpr/rqad,rqbd->rab/dot_general | solution.py:78
  332.7 4.4 %fusion.134 = f32[8,128,128]{2,1,0:T(8,128)} fusion(bf16[8,40,128,128]{3,2,1,0:T(8,128)(2,1)} %get-tuple-element.461, s32[]{:T(128)S(6)} %select_n.83, f32[8,128,128]{2,1,0:T(8,128)} %get-tuple-element.452, bf16[8,128,128]{2,1,0:T(8,128)(2,1)S(1)} %get-tuple-element.462, pred[]{:T(512)S(6)} %compare.11), kind=kOutput, calls=%fused_computation.29.clone.1 | convolution fusion | flops 538181632 | bytes 5506560 | tf_op jit(solution)/shard_map/while/body/eval_jaxpr/rqad,rqbd->rab/dot_general | solution.py:78
  337.0 4.4 %fusion.134 = f32[8,128,128]{2,1,0:T(8,128)} fusion(bf16[8,40,128,128]{3,2,1,0:T(8,128)(2,1)} %get-tuple-element.461, s32[]{:T(128)S(6)} %select_n.83, f32[8,128,128]{2,1,0:T(8,128)} %get-tuple-element.452, bf16[8,128,128]{2,1,0:T(8,128)(2,1)S(1)} %get-tuple-element.462, pred[]{:T(512)S(6)} %compare.11), kind=kOutput, calls=%fused_computation.29.clone.1 | convolution fusion | flops 538181632 | bytes 5506560 | tf_op jit(solution)/shard_map/while/body/eval_jaxpr/rqad,rqbd->rab/dot_general | solution.py:78
  341.4 49.4 %all-to-all-done.4 = bf16[32,3,128,128]{3,2,1,0:T(8,128)(2,1)S(1)} async-done(((bf16[32,3,128,128]{3,2,1,0:T(8,128)(2,1)}), bf16[32,3,128,128]{3,2,1,0:T(8,128)(2,1)S(1)}, u32[]{:S(2)}, u32[]{:S(2)}) %all-to-all-start.4) | async-done | bytes 3145760 | tf_op jit(solution)/shard_map/all_to_all | solution.py:69
  393.5 6.0 %convert_reduce_fusion = f32[8,128,128]{2,1,0:T(8,128)S(1)} fusion(bf16[8,12,128,128]{3,2,1,0:T(8,128)(2,1)} %convolution_convert_fusion, f32[8,12]{1,0:T(8,128)S(1)} %convert_element_type.103, bf16[8,12,128,128]{3,2,1,0:T(8,128)(2,1)} %bitcast.93), kind=kOutput, calls=%fused_computation.32 | convolution fusion | flops 813039616 | bytes 6816128 | tf_op jit(solution)/shard_map/rcad,rced->rcae/dot_general | solution.py:94
  (76 shorter events, 69.7 us)
Async XLA Ops:
  2.9 14.4 %all-to-all-start = ((s32[32,1,3]{2,1,0:T(1,128)}), s32[32,1,3]{2,1,0:T(1,128)S(1)}, u32[]{:S(2)}, u32[]{:S(2)}) async-start(s32[32,1,3]{2,1,0:T(1,128)} %copy.46), calls=%async_computation | async-start | bytes 32768 | tf_op jit(solution)/shard_map/all_to_all | solution.py:51
  20.8 3.7 copy-start.7
  20.8 75.1 %all-to-all-start.2 = ((bf16[32,3,128,128]{3,2,1,0:T(8,128)(2,1)}), bf16[32,3,128,128]{3,2,1,0:T(8,128)(2,1)}, u32[]{:S(2)}, u32[]{:S(2)}) async-start(bf16[32,3,128,128]{3,2,1,0:T(8,128)(2,1)} %broadcast_select_fusion.3), calls=%async_computation.2 | async-start | bytes 6291456 | tf_op jit(solution)/shard_map/all_to_all | solution.py:69
  32.9 67.2 %copy-start.9 = (s32[8,12]{1,0:T(8,128)S(1)}, s32[8,12]{1,0:T(8,128)}, u32[]{:S(2)}) copy-start(s32[8,12]{1,0:T(8,128)} %param.17) | copy-start | bytes 1156
  32.9 67.3 %copy-start.11 = (bf16[8,12]{1,0:T(8,128)(2,1)S(1)}, bf16[8,12]{1,0:T(8,128)(2,1)}, u32[]{:S(2)}) copy-start(bf16[8,12]{1,0:T(8,128)(2,1)} %param.23) | copy-start | bytes 580
  95.9 109.2 %all-to-all-start.1 = ((bf16[32,3,192,128]{3,2,1,0:T(8,128)(2,1)}), bf16[32,3,192,128]{3,2,1,0:T(8,128)(2,1)}, u32[]{:S(2)}, u32[]{:S(2)}) async-start(bf16[32,3,192,128]{3,2,1,0:T(8,128)(2,1)} %broadcast_select_fusion), calls=%async_computation.1 | async-start | bytes 9437184 | tf_op jit(solution)/shard_map/all_to_all | solution.py:54
  217.0 6.0 %copy-start = (bf16[8,128,128]{2,1,0:T(8,128)(2,1)S(1)}, bf16[8,128,128]{2,1,0:T(8,128)(2,1)}, u32[]{:S(2)}) copy-start(bf16[8,128,128]{2,1,0:T(8,128)(2,1)} %param.19) | copy-start | bytes 786436
  217.0 6.0 %copy-start.8 = (f32[8,128]{1,0:T(8,128)S(1)}, f32[8,128]{1,0:T(8,128)}, u32[]{:S(2)}) copy-start(f32[8,128]{1,0:T(8,128)} %param.21) | copy-start | bytes 12292
  217.0 6.0 %copy-start.10 = (f32[8]{0:T(128)S(1)}, f32[8]{0:T(128)}, u32[]{:S(2)}) copy-start(f32[8]{0:T(128)} %param.22) | copy-start | bytes 100
  227.3 75.3 %all-to-all-start.3 = ((bf16[32,3,128,128]{3,2,1,0:T(8,128)(2,1)}), bf16[32,3,128,128]{3,2,1,0:T(8,128)(2,1)S(1)}, u32[]{:S(2)}, u32[]{:S(2)}) async-start(bf16[32,3,128,128]{3,2,1,0:T(8,128)(2,1)} %broadcast_select_fusion.2), calls=%async_computation.3 | async-start | bytes 6291456 | tf_op jit(solution)/shard_map/all_to_all | solution.py:69
  305.3 6.1 %copy-start.1 = (bf16[8,128,128]{2,1,0:T(8,128)(2,1)S(1)}, bf16[8,128,128]{2,1,0:T(8,128)(2,1)}, u32[]{:S(2)}) copy-start(bf16[8,128,128]{2,1,0:T(8,128)(2,1)} %param.19) | copy-start | bytes 786436
  305.3 6.1 %copy-start.3 = (f32[8,128,128]{2,1,0:T(8,128)S(1)}, f32[8,128,128]{2,1,0:T(8,128)}, u32[]{:S(2)}) copy-start(f32[8,128,128]{2,1,0:T(8,128)} %get-tuple-element.317) | copy-start | bytes 1572868
  305.3 6.1 %copy-start.5 = (f32[8,128,128]{2,1,0:T(8,128)S(1)}, f32[8,128,128]{2,1,0:T(8,128)}, u32[]{:S(2)}) copy-start(f32[8,128,128]{2,1,0:T(8,128)} %get-tuple-element.243) | copy-start | bytes 1572868
  315.6 75.2 %all-to-all-start.4 = ((bf16[32,3,128,128]{3,2,1,0:T(8,128)(2,1)}), bf16[32,3,128,128]{3,2,1,0:T(8,128)(2,1)S(1)}, u32[]{:S(2)}, u32[]{:S(2)}) async-start(bf16[32,3,128,128]{3,2,1,0:T(8,128)(2,1)} %broadcast_select_fusion.1), calls=%async_computation.4 | async-start | bytes 6291456 | tf_op jit(solution)/shard_map/all_to_all | solution.py:69
  393.5 6.1 %copy-start.2 = (bf16[8,128,128]{2,1,0:T(8,128)(2,1)S(1)}, bf16[8,128,128]{2,1,0:T(8,128)(2,1)}, u32[]{:S(2)}) copy-start(bf16[8,128,128]{2,1,0:T(8,128)(2,1)} %param.19) | copy-start | bytes 786436
  393.5 6.1 %copy-start.4 = (f32[8,128,128]{2,1,0:T(8,128)S(1)}, f32[8,128,128]{2,1,0:T(8,128)}, u32[]{:S(2)}) copy-start(f32[8,128,128]{2,1,0:T(8,128)} %get-tuple-element.315) | copy-start | bytes 1572868
  393.5 6.1 %copy-start.6 = (f32[8,128,128]{2,1,0:T(8,128)S(1)}, f32[8,128,128]{2,1,0:T(8,128)}, u32[]{:S(2)}) copy-start(f32[8,128,128]{2,1,0:T(8,128)} %get-tuple-element.244) | copy-start | bytes 1572868
where the time goes:
time: 401 us
  waiting for transfers between devices  249 us (62%)
  matrix products  86.1 us (21%)
  local copies, waits for them, and re-layouts  24.8 us (6%)
  starting transfers between devices  23.1 us (6%)
  other arithmetic  17.5 us (4%)
    all_to_all x3, waiting for transfers between devices, shards(): lax.all_to_all(sent_rows, 'pairs', split_axis=0, concat_axis=0, tiled=True)  162 us
    all_to_all x1, waiting for transfers between devices, shards(): lax.all_to_all(sent_basis, 'pairs', split_axis=0, concat_axis=0, tiled=True)  81.9 us
    dot_general x15, matrix products, add_group(): jnp.einsum('rqad,rqbd->rab', ladder_half, factors, preferred_element_type...  61.9 us
    dot_general x3, matrix products, shards(): jnp.einsum('rcad,rced->rcae', left_half, margin, preferred_element_type=j...  18.1 us
    all_to_all x3, starting transfers between devices, shards(): lax.all_to_all(sent_rows, 'pairs', split_axis=0, concat_axis=0, tiled=True)  11.7 us
    select_n x4, other arithmetic, gather_rows(): return jnp.where(extended, picked, jnp.zeros_like(picked))  10.6 us
    gather x3, local copies, waits for them, and re-layouts, shards(): arrived_amps.reshape(peer_count * slot_count, orbitals, orbitals)[flat_slot]  9.93 us
  transfers between devices with their start and end apart: 5, of which 5 were waited for; matrix products, arithmetic and copies ran while one was open for 19% of the time, Pallas kernels for 0%

commit v1 on v0

--- a/solution.py
+++ b/solution.py
@@ -7,12 +7,6 @@
 
 
 level_shift = 0.3
-
-
-def gather_rows(source_rows, chosen, usable):
-    picked = source_rows[jnp.clip(chosen, 0, source_rows.shape[0] - 1)]
-    extended = usable.reshape(usable.shape + (1,) * (picked.ndim - usable.ndim))
-    return jnp.where(extended, picked, jnp.zeros_like(picked))
 
 
 def shards(
@@ -26,34 +20,16 @@
     occ_energy,
     coupling_fock,
 ):
-    peer_count = lax.axis_size("pairs")
     own_pairs, domain, orbitals = pno_basis.shape
     fitted = ladder_factor.shape[1]
     partners = partner_owner.shape[1]
     listed = own_pairs * partners
-    slot_count = max(2, (listed + peer_count - 1) // peer_count)
     columns = lax.broadcasted_iota(jnp.int32, (own_pairs, orbitals), 1)
     live_cols = (columns < pno_count[:, None]).astype(jnp.float32)
     masked_basis = pno_basis * live_cols[:, None, :].astype(jnp.bfloat16)
-    flat_owner = partner_owner.reshape(listed)
-    flat_local = partner_local.reshape(listed)
-    owner_onehot = (
-        flat_owner[:, None] == lax.broadcasted_iota(jnp.int32, (listed, peer_count), 1)
-    ).astype(jnp.int32)
-    before = jnp.cumsum(owner_onehot, axis=0) - owner_onehot
-    slot_rank = jnp.sum(before * owner_onehot, axis=1)
-    flat_slot = flat_owner * slot_count + slot_rank
-    slot_onehot = (
-        slot_rank[:, None] == lax.broadcasted_iota(jnp.int32, (listed, slot_count), 1)
-    ).astype(jnp.int32)
-    labelled = slot_onehot * (flat_local + 1)[:, None]
-    wanted = jnp.sum(owner_onehot[:, :, None] * labelled[:, None, :], axis=0) - 1
-    asked_rows = lax.all_to_all(wanted, "pairs", split_axis=0, concat_axis=0, tiled=True)
-    asked_usable = asked_rows >= 0
-    sent_basis = gather_rows(masked_basis, asked_rows, asked_usable)
-    arrived_basis = lax.all_to_all(sent_basis, "pairs", split_axis=0, concat_axis=0, tiled=True)
-    partner_basis = arrived_basis.reshape(peer_count * slot_count, domain, orbitals)[flat_slot]
-    partner_basis = partner_basis.reshape(own_pairs, partners, domain, orbitals)
+    partner = (partner_owner * own_pairs + partner_local).reshape(listed)
+    every_basis = lax.all_gather(masked_basis, "pairs", axis=0, tiled=True)
+    partner_basis = every_basis[partner].reshape(own_pairs, partners, domain, orbitals)
     margin = jnp.einsum(
         "rva,rcvb->rcab", masked_basis, partner_basis, preferred_element_type=jnp.float32
     ).astype(jnp.bfloat16)
@@ -65,8 +41,7 @@
     group_width = 8
     for iteration in range(ITERS):
         sent_amps = amplitudes.astype(jnp.bfloat16)
-        sent_rows = gather_rows(sent_amps, asked_rows, asked_usable)
-        arrived_amps = lax.all_to_all(sent_rows, "pairs", split_axis=0, concat_axis=0, tiled=True)
+        every_amps = lax.all_gather(sent_amps, "pairs", axis=0, tiled=True)
 
         def add_group(group_index, total):
             factors = lax.dynamic_slice_in_dim(
@@ -85,7 +60,7 @@
             add_group,
             jnp.zeros((own_pairs, orbitals, orbitals), jnp.float32),
         )
-        partner_amps = arrived_amps.reshape(peer_count * slot_count, orbitals, orbitals)[flat_slot]
+        partner_amps = every_amps[partner]
         partner_amps = partner_amps.reshape(own_pairs, partners, orbitals, orbitals)
         left_half = jnp.einsum(
             "rcab,rcbd->rcad", margin, partner_amps, preferred_element_type=jnp.float32

time: 401 us -> 394 us (0.983)
  starting transfers between devices: 23.1 us -> 0.31 us
  between operations: 0.3 us -> 13.2 us
  waiting for transfers between devices: 249 us -> 261 us
  matrix products: 86.1 us -> 79.9 us
    all_gather x0 -> x4, waiting for transfers between devices: none -> 261 us  [the longest x3 169 us: shards(): every_amps = lax.all_gather(sent_amps, 'pairs', axis=0, tiled=True)]
    all_to_all x5 -> x0, waiting for transfers between devices: 249 us -> none  [the longest x3 162 us: shards(): lax.all_to_all(sent_rows, 'pairs', split_axis=0, concat_axis=0, tiled=True)]
    all_to_all x5 -> x0, starting transfers between devices: 23.1 us -> none  [the longest x3 11.7 us: shards(): lax.all_to_all(sent_rows, 'pairs', split_axis=0, concat_axis=0, tiled=True)]
    select_n x6 -> x1, other arithmetic: 10.6 us -> 0.01 us  [shards(): every_basis[partner].reshape(own_pairs, partners, domain, orbitals)]
    dot_general x15, matrix products: 61.9 us -> 56.1 us  [add_group(): jnp.einsum('rqad,rqbd->rab', ladder_half, factors, preferred_element_type...]
    gather x8 -> x4, local copies, waits for them, and re-layouts: 22.7 us -> 21.6 us  [the longest x3 13.6 us: shards(): partner_amps = every_amps[partner]]
  transfers between devices with their start and end apart: 5 -> 4, of which waited for: 5 -> 4; matrix products, arithmetic and copies ran while one was open for 19% -> 16% of each run, Pallas kernels for 0% -> 0%
where the time goes in v1:
time: 394 us; the launch traced here: 393 us
  waiting for transfers between devices  261 us (66%)
  matrix products  79.9 us (20%)
  local copies, waits for them, and re-layouts  24 us (6%)
  other arithmetic  14.1 us (4%)
  between operations  13.2 us (3%)
    all_gather x3, waiting for transfers between devices, shards(): every_amps = lax.all_gather(sent_amps, 'pairs', axis=0, tiled=True)  169 us
    all_gather x1, waiting for transfers between devices, shards(): every_basis = lax.all_gather(masked_basis, 'pairs', axis=0, tiled=True)  92.1 us
    dot_general x15, matrix products, add_group(): jnp.einsum('rqad,rqbd->rab', ladder_half, factors, preferred_element_type...  56.1 us
    dot_general x3, matrix products, shards(): jnp.einsum('rcad,rced->rcae', left_half, margin, preferred_element_type=j...  17.7 us
    gather x3, local copies, waits for them, and re-layouts, shards(): partner_amps = every_amps[partner]  13.6 us
    gather x1, local copies, waits for them, and re-layouts, shards(): every_basis[partner].reshape(own_pairs, partners, domain, orbitals)  7.96 us
  transfers between devices with their start and end apart: 4, of which 4 were waited for; matrix products, arithmetic and copies ran while one was open for 16% of the time, Pallas kernels for 0%

profile of v1, /device:TPU:0, one launch (start us, length us, event | category | flops | bytes accessed | tf_op | source)
XLA Modules:
  0.0 393.3 jit_solution(389389838037851745)
XLA Ops:
  13.3 18.9 %while.42 = (s32[]{:T(128)}, f32[8,128,128]{2,1,0:T(8,128)S(1)}, bf16[8,40,128,128]{3,2,1,0:T(8,128)(2,1)}, bf16[8,128,128]{2,1,0:T(8,128)(2,1)}, s32[]{:T(128)}, /*index=5*/s32[]{:T(128)}, s32[]{:T(128)}, s32[]{:T(128)}) while((s32[]{:T(128)}, f32[8,128,128]{2,1,0:T(8,128)S(1)}, bf16[8,40,128,128]{3,2,1,0:T(8,128)(2,1)}, ...), condition=%wide.region_2.0_spmd.clone, body=%wide.region_1.0_spmd.clone.sunk | while | flops 538181632 | bytes 5506700 | solution.py:57
  17.1 3.7 fusion.122
  20.8 3.9 fusion.122
  24.7 3.7 fusion.122
  33.0 57.0 %all-gather.7.cloned.1.call-done = bf16[256,128,128]{2,1,0:T(8,128)(2,1)} async-done(((bf16[8,128,128]{2,1,0:T(8,128)(2,1)}), bf16[256,128,128]{2,1,0:T(8,128)(2,1)}) %all-gather.7.cloned.1.call-update) | async-done | bytes 8388624 | tf_op jit(solution)/shard_map/all_gather | solution.py:44
  90.0 4.5 %gather_fusion.1 = bf16[96,128,128]{2,1,0:T(8,128)(2,1)S(1)} fusion(bf16[256,128,128]{2,1,0:T(8,128)(2,1)} %all-gather.7.cloned.1.call-done, s32[1024]{0:T(1024)S(1)} %pad_clamp_fusion), kind=kCustom, calls=%fused_computation.1 | custom fusion | bytes 6291840 | tf_op jit(solution)/shard_map/gather | solution.py:63
  94.5 92.1 %all-gather.5.cloned.1.call-done = bf16[256,192,128]{2,1,0:T(8,128)(2,1)} async-done(((bf16[8,192,128]{2,1,0:T(8,128)(2,1)}), bf16[256,192,128]{2,1,0:T(8,128)(2,1)}) %all-gather.5.cloned.1.call-update) | async-done | bytes 12582928 | tf_op jit(solution)/shard_map/all_gather | solution.py:31
  186.7 8.0 %gather_fusion = bf16[96,192,128]{2,1,0:T(8,128)(2,1)} fusion(bf16[256,192,128]{2,1,0:T(8,128)(2,1)} %all-gather.5.cloned.1.call-done, s32[1024]{0:T(1024)S(1)} %pad_clamp_fusion), kind=kCustom, calls=%fused_computation | custom fusion | bytes 9437568 | tf_op jit(solution)/shard_map/gather | solution.py:32
  194.6 6.2 %convolution_convert_fusion = bf16[8,12,128,128]{3,2,1,0:T(8,128)(2,1)} fusion(bf16[8,12,192,128]{3,2,1,0:T(8,128)(2,1)} %bitcast.66, bf16[8,192,128]{2,1,0:T(8,128)(2,1)S(1)} %copy-done.1), kind=kOutput, calls=%fused_computation.43 | convolution fusion | flops 605552640 | bytes 8257536 | tf_op jit(solution)/shard_map/rva,rcvb->rcab/dot_general | solution.py:33
  200.8 5.9 %convert_reduce_fusion.2 = f32[8,128,128]{2,1,0:T(8,128)} fusion(bf16[8,12,128,128]{3,2,1,0:T(8,128)(2,1)} %convolution_convert_fusion, f32[8,12]{1,0:T(8,128)} %convert_element_type.94, bf16[8,12,128,128]{3,2,1,0:T(8,128)(2,1)S(1)} %bitcast.67), kind=kOutput, calls=%fused_computation.32 | convolution fusion | flops 813039616 | bytes 6816128 | tf_op jit(solution)/shard_map/rcad,rced->rcae/dot_general | solution.py:69
  209.4 18.8 %while.43 = (s32[]{:T(128)}, f32[8,128,128]{2,1,0:T(8,128)S(1)}, bf16[8,40,128,128]{3,2,1,0:T(8,128)(2,1)}, bf16[8,128,128]{2,1,0:T(8,128)(2,1)}, s32[]{:T(128)}, /*index=5*/s32[]{:T(128)}, s32[]{:T(128)}, s32[]{:T(128)}) while((s32[]{:T(128)}, f32[8,128,128]{2,1,0:T(8,128)S(1)}, bf16[8,40,128,128]{3,2,1,0:T(8,128)(2,1)}, ...), condition=%wide.region_5.0_spmd.clone, body=%wide.region_4.0_spmd.clone.sunk | while | flops 538181632 | bytes 5506700 | solution.py:57
  216.9 3.8 fusion.127
  220.7 3.7 fusion.127
  224.5 3.7 fusion.127
  229.1 55.9 %all-gather.9.cloned.1.call-done = bf16[256,128,128]{2,1,0:T(8,128)(2,1)} async-done(((bf16[8,128,128]{2,1,0:T(8,128)(2,1)}), bf16[256,128,128]{2,1,0:T(8,128)(2,1)}) %all-gather.9.cloned.1.call-update) | async-done | bytes 8388624 | tf_op jit(solution)/shard_map/all_gather | solution.py:44
  285.0 4.5 %gather_fusion.2 = bf16[96,128,128]{2,1,0:T(8,128)(2,1)S(1)} fusion(bf16[256,128,128]{2,1,0:T(8,128)(2,1)} %all-gather.9.cloned.1.call-done, s32[1024]{0:T(1024)S(1)} %pad_clamp_fusion), kind=kCustom, calls=%fused_computation.2 | custom fusion | bytes 6291840 | tf_op jit(solution)/shard_map/gather | solution.py:63
  289.5 5.9 %convert_reduce_fusion.1 = f32[8,128,128]{2,1,0:T(8,128)} fusion(bf16[8,12,128,128]{3,2,1,0:T(8,128)(2,1)} %convolution_convert_fusion, f32[8,12]{1,0:T(8,128)S(1)} %copy-done.7, bf16[8,12,128,128]{3,2,1,0:T(8,128)(2,1)S(1)} %bitcast.69), kind=kOutput, calls=%fused_computation.30 | convolution fusion | flops 813039616 | bytes 6816128 | tf_op jit(solution)/shard_map/rcad,rced->rcae/dot_general | solution.py:69
  298.0 18.8 %while.44 = (s32[]{:T(128)}, f32[8,128,128]{2,1,0:T(8,128)S(1)}, bf16[8,40,128,128]{3,2,1,0:T(8,128)(2,1)}, bf16[8,128,128]{2,1,0:T(8,128)(2,1)}, s32[]{:T(128)}, /*index=5*/s32[]{:T(128)}, s32[]{:T(128)}, s32[]{:T(128)}) while((s32[]{:T(128)}, f32[8,128,128]{2,1,0:T(8,128)S(1)}, bf16[8,40,128,128]{3,2,1,0:T(8,128)(2,1)}, ...), condition=%wide.region_8.0_spmd.clone, body=%wide.region_7.0_spmd.clone.sunk | while | flops 538181632 | bytes 5506700 | solution.py:57
  305.6 3.8 fusion.132
  309.4 3.7 fusion.132
  313.1 3.7 fusion.132
  317.7 56.2 %all-gather.11.cloned.1.call-done = bf16[256,128,128]{2,1,0:T(8,128)(2,1)} async-done(((bf16[8,128,128]{2,1,0:T(8,128)(2,1)}), bf16[256,128,128]{2,1,0:T(8,128)(2,1)}) %all-gather.11.cloned.1.call-update) | async-done | bytes 8388624 | tf_op jit(solution)/shard_map/all_gather | solution.py:44
  373.9 4.5 %gather_fusion.3 = bf16[96,128,128]{2,1,0:T(8,128)(2,1)S(1)} fusion(bf16[256,128,128]{2,1,0:T(8,128)(2,1)} %all-gather.11.cloned.1.call-done, s32[1024]{0:T(1024)S(1)} %pad_clamp_fusion), kind=kCustom, calls=%fused_computation.3 | custom fusion | bytes 6291840 | tf_op jit(solution)/shard_map/gather | solution.py:63
  378.4 5.9 %convert_reduce_fusion = f32[8,128,128]{2,1,0:T(8,128)} fusion(bf16[8,12,128,128]{3,2,1,0:T(8,128)(2,1)} %convolution_convert_fusion, f32[8,12]{1,0:T(8,128)S(1)} %copy-done.7, bf16[8,12,128,128]{3,2,1,0:T(8,128)(2,1)S(1)} %bitcast.68), kind=kOutput, calls=%fused_computation.28 | convolution fusion | flops 813039616 | bytes 6816128 | tf_op jit(solution)/shard_map/rcad,rced->rcae/dot_general | solution.py:69
  (44 shorter events, 39.3 us)
Async XLA Ops:
  6.5 83.5 %all-gather.7.cloned.1.call-start = ((), (), s32[]{:S(2)}) async-start(), calls=%async_computation.1 | async-start | bytes 8650752 | tf_op jit(solution)/shard_map/all_gather | solution.py:44
  9.3 177.3 %all-gather.5.cloned.1.call-start = ((), (), s32[]{:S(2)}) async-start(), calls=%async_computation | async-start | bytes 12976128 | tf_op jit(solution)/shard_map/all_gather | solution.py:31
  11.2 273.8 %all-gather.9.cloned.1.call-start = ((), (), s32[]{:S(2)}) async-start(), calls=%async_computation.2 | async-start | bytes 8650752 | tf_op jit(solution)/shard_map/all_gather | solution.py:44
  32.2 0.8 copy-start.2
  94.5 100.1 %copy-start.1 = (bf16[8,192,128]{2,1,0:T(8,128)(2,1)S(1)}, bf16[8,192,128]{2,1,0:T(8,128)(2,1)}, u32[]{:S(2)}) copy-start(bf16[8,192,128]{2,1,0:T(8,128)(2,1)} %broadcast_multiply_fusion) | copy-start | bytes 1179652
  200.8 5.9 %copy-start = (bf16[8,128,128]{2,1,0:T(8,128)(2,1)S(1)}, bf16[8,128,128]{2,1,0:T(8,128)(2,1)}, u32[]{:S(2)}) copy-start(bf16[8,128,128]{2,1,0:T(8,128)(2,1)} %param.19) | copy-start | bytes 786436
  200.8 5.9 %copy-start.5 = (f32[8,128]{1,0:T(8,128)S(1)}, f32[8,128]{1,0:T(8,128)}, u32[]{:S(2)}) copy-start(f32[8,128]{1,0:T(8,128)} %param.21) | copy-start | bytes 12292
  200.8 5.9 %copy-start.6 = (f32[8]{0:T(128)S(1)}, f32[8]{0:T(128)}, u32[]{:S(2)}) copy-start(f32[8]{0:T(128)} %param.22) | copy-start | bytes 100
  209.2 164.7 %all-gather.11.cloned.1.call-start = ((), (), s32[]{:S(2)}) async-start(), calls=%async_computation.3 | async-start | bytes 8650752 | tf_op jit(solution)/shard_map/all_gather | solution.py:44
  228.3 0.8 copy-start.3
  229.1 60.5 %copy-start.7 = (f32[8,12]{1,0:T(8,128)S(1)}, f32[8,12]{1,0:T(8,128)}, u32[]{:S(2)}) copy-start(f32[8,12]{1,0:T(8,128)} %convert_element_type.94) | copy-start | bytes 1156
  316.9 0.8 copy-start.4
Sparse Core Ops, SparseCore 0:
  10.2 79.7 all-gather.6
  92.9 93.7 all-gather.4
  209.3 75.6 all-gather.8
  298.2 75.6 all-gather.10

commit v2 on v1

--- a/solution.py
+++ b/solution.py
@@ -1,15 +1,335 @@
+import functools
 import jax
 import jax.numpy as jnp
 from jax import lax
+from jax.experimental import pallas as pl
+from jax.experimental.pallas import tpu as pltpu
 from jax.sharding import PartitionSpec as P
 
 ITERS = 3
 
 
 level_shift = 0.3
-
-
-def shards(
+VMEM_BYTES = 67043328
+MESH = pl.DeviceIdType.MESH
+
+
+def contract(a, b, da, db):
+    return lax.dot_general(a, b, (((da,), (db,)), ((), ())), preferred_element_type=jnp.float32)
+
+
+def kernel(
+    n, basis_ref, count_ref, owner_ref, local_ref, exchange_ref, ladder_hbm, energy_ref,
+    energy_cols_ref, occ_ref, fock_ref, out_ref,
+    all_basis, amps_a, amps_b, factors, margin, ladder,
+    load_sem, recv_sem, recv_sib, send_z, send_near, send_sib,
+):
+    own_pairs, domain, orbitals = basis_ref.shape
+    fitted = factors.shape[1]
+    partners = owner_ref.shape[1]
+    depth = n // 8
+    stride = 8
+    me = lax.axis_index("pairs")
+    core = me % 2
+    line = me // stride
+    near = 2 + 2 * core
+    far = 4 - 2 * core
+    shift_near = near * (1 - 2 * ((me // 2 % 2) * (1 - core) + (me // 4 % 2) * core))
+    shift_far = far * (1 - 2 * ((me // 4 % 2) * (1 - core) + (me // 2 % 2) * core))
+    near_dev = me + shift_near
+    far_dev = me + shift_far
+    sibling = me + 1 - 2 * core
+    bases = (me, near_dev, far_dev, me + shift_near + shift_far)
+    tail = own_pairs // 4
+    spans = ((0, own_pairs - tail), (own_pairs - tail, tail))
+    rounds = (all_basis, amps_a, amps_b, amps_a)
+
+    loads = [
+        pltpu.make_async_copy(ladder_hbm.at[p], factors.at[p], load_sem.at[p])
+        for p in range(own_pairs)
+    ]
+    for load in loads:
+        load.start()
+
+    def remote(r, t, owner, dev, ssem, rsem):
+        lo, cnt = spans[t]
+        view = rounds[r].at[owner, pl.ds(lo, cnt)]
+        return pltpu.make_async_remote_copy(
+            src_ref=view, dst_ref=view, send_sem=ssem, recv_sem=rsem,
+            device_id=(dev,), device_id_type=MESH,
+        )
+
+    def send_line(r, t, owner, up):
+        def go():
+            remote(r, t, owner, me + stride * (1 if up else -1),
+                   send_z.at[r % 2, int(up), t, owner // 2], recv_sem.at[r, t, owner // 2]).start()
+        pl.when((line < depth - 1) if up else (line > 0))(go)
+
+    def send_to(r, t, owner, which):
+        dev = (near_dev, far_dev)[which]
+        remote(r, t, owner, dev, send_near.at[r % 2, t, which], recv_sem.at[r, t, owner // 2]).start()
+
+    def send_sibling(r, t, owner):
+        remote(r, t, owner, sibling, send_sib.at[r % 2, t], recv_sib.at[r, t]).start()
+
+    def forward(r, t, owner, via, up=None):
+        if t == 0:
+            if via in ("own", "line"):
+                if up is None or up is False:
+                    send_line(r, t, owner, False)
+                if up is None or up is True:
+                    send_line(r, t, owner, True)
+                send_to(r, t, owner, 0)
+            if via in ("own", "line", "near"):
+                send_to(r, t, owner, 1)
+        else:
+            if via == "own":
+                send_to(r, t, owner, 0)
+            if via in ("own", "near"):
+                send_to(r, t, owner, 1)
+            if up is None or up is False:
+                send_line(r, t, owner, False)
+            if up is None or up is True:
+                send_line(r, t, owner, True)
+        send_sibling(r, t, owner)
+
+    def arrive(r, t, owner, via, up=None):
+        remote(r, t, owner, sibling, send_sib.at[r % 2, t], recv_sem.at[r, t, owner // 2]).wait_recv()
+        forward(r, t, owner, via, up)
+
+    def start_own(r):
+        for t in (0, 1):
+            forward(r, t, me, "own")
+
+    vias = ("own", "near", "far", "far")
+
+    def steps(r):
+        found = []
+
+        def at(t, b, k, up):
+            def go():
+                if k == 0:
+                    arrive(r, t, bases[b], vias[b])
+                else:
+                    place = line + (k if up is False else -k)
+                    owner = bases[b] + stride * (k if up is False else -k)
+
+                    def inner():
+                        if t == 0:
+                            arrive(r, 0, owner, "line" if b == 0 else vias[b], up if b == 0 else None)
+                        else:
+                            arrive(r, 1, owner, "line", up)
+                    pl.when((place >= 0) & (place < depth))(inner)
+            found.append(go)
+
+        for k in range(depth):
+            for b in range(4):
+                if k == 0:
+                    if b == 0:
+                        continue
+                    at(1, b, 0, None)
+                    at(0, b, 0, None)
+                else:
+                    for t in (0, 1):
+                        for up in (True, False):
+                            at(t, b, k, up)
+        return found
+
+    def run(r, pieces):
+        todo = steps(r)
+        done = 0
+        for i, step in enumerate(todo):
+            step()
+            upto = len(pieces) * (i + 1) // len(todo)
+            for piece in pieces[done:upto]:
+                piece()
+            done = upto
+        whole(r, 0, n // 2, recv_sib.at[r, 0])
+        whole(r, 1, n // 2, recv_sib.at[r, 1])
+
+    def whole(r, t, number, sem):
+        lo, cnt = spans[t]
+        view = rounds[r].at[pl.ds(0, number), pl.ds(lo, cnt)]
+        pltpu.make_async_copy(view, view, sem).wait()
+
+    def finish_sends(r):
+        for t in (0, 1):
+            whole(r, t, depth if t == 0 else 1, send_near.at[r % 2, t, 0])
+            whole(r, t, 2 * depth if t == 0 else 2, send_near.at[r % 2, t, 1])
+            whole(r, t, n // 2, send_sib.at[r % 2, t])
+            for b in range(1 if t == 0 else 4):
+                for up in (True, False):
+                    for j in range(depth):
+                        owner = bases[b] + stride * (j - line)
+
+                        def go(owner=owner, up=up, t=t):
+                            remote(r, t, owner, sibling, send_z.at[r % 2, int(up), t, owner // 2],
+                                   recv_sem.at[r, t, owner // 2]).wait_send()
+                        pl.when(((line < depth - 1) & (j <= line)) if up else ((line > 0) & (j >= line)))(go)
+
+    lanes = lax.broadcasted_iota(jnp.int32, (orbitals, orbitals), 1)
+    rows = lax.broadcasted_iota(jnp.int32, (orbitals, orbitals), 0)
+
+    def pair_terms(p):
+        esum = energy_cols_ref[:, p : p + 1] + energy_ref[p : p + 1, :] - occ_ref[p]
+        count = count_ref[p]
+        live = (lanes < count) & (rows < count)
+        driving = jnp.where(live, exchange_ref[p].astype(jnp.float32), 0.0)
+        return esum, esum + level_shift, driving
+
+    basis_lanes = lax.broadcasted_iota(jnp.int32, (domain, orbitals), 1)
+    for p in range(own_pairs):
+        all_basis[me, p] = jnp.where(
+            basis_lanes < count_ref[p], basis_ref[p].astype(jnp.float32), 0.0
+        ).astype(jnp.bfloat16)
+        esum, divisor, driving = pair_terms(p)
+        first = -driving / divisor
+        out_ref[p] = first
+        rounds[1][me, p] = first.astype(jnp.bfloat16)
+
+    barrier = pltpu.get_barrier_semaphore()
+    for dev in (near_dev, far_dev, sibling):
+        pl.semaphore_signal(barrier, inc=1, device_id=(dev,), device_id_type=MESH)
+
+    @pl.when(line > 0)
+    def _():
+        pl.semaphore_signal(barrier, inc=1, device_id=(me - stride,), device_id_type=MESH)
+
+    @pl.when(line < depth - 1)
+    def _():
+        pl.semaphore_signal(barrier, inc=1, device_id=(me + stride,), device_id_type=MESH)
+
+    @pl.when((line > 0) & (line < depth - 1))
+    def _():
+        pl.semaphore_wait(barrier, 5)
+
+    @pl.when((line == 0) | (line == depth - 1))
+    def _():
+        pl.semaphore_wait(barrier, 4)
+
+    group = 10 if fitted % 10 == 0 else 2
+
+    def ladder_piece(r, p, first):
+        def piece():
+            if first:
+                loads[p].wait()
+            held = rounds[r][me, p]
+
+            def body(g, total):
+                for q in range(0, group, 2):
+                    one = factors[p, g * group + q]
+                    two = factors[p, g * group + q + 1]
+                    half = jnp.concatenate(
+                        [contract(one, held, 1, 0), contract(two, held, 1, 0)], axis=1
+                    ).astype(jnp.bfloat16)
+                    total = total + contract(half, jnp.concatenate([one, two], axis=1), 1, 1)
+                return total
+
+            ladder[p] = lax.fori_loop(
+                0, fitted // group, body, jnp.zeros((orbitals, orbitals), jnp.float32)
+            )
+        return piece
+
+    def margin_piece(p):
+        def piece():
+            flipped = jnp.transpose(all_basis[me, p].astype(jnp.float32)).astype(jnp.bfloat16)
+            for c in range(partners):
+                other = all_basis[owner_ref[p, c], local_ref[p, c]]
+                margin[p, :, c * orbitals : (c + 1) * orbitals] = contract(
+                    flipped, other, 1, 0
+                ).astype(jnp.bfloat16)
+        return piece
+
+    def couple(r, p):
+        amps = rounds[r]
+        total = ladder[p]
+        for c in range(0, partners, 2):
+            both = margin[p, :, c * orbitals : (c + 2) * orbitals]
+            lefts = []
+            for d in (c, c + 1):
+                block = amps[owner_ref[p, d], local_ref[p, d]]
+                lefts.append(
+                    contract(both[:, (d - c) * orbitals : (d - c + 1) * orbitals], block, 1, 0)
+                    * fock_ref[p, d]
+                )
+            left = jnp.concatenate(lefts, axis=1).astype(jnp.bfloat16)
+            total = total + contract(left, both, 1, 1)
+        esum, divisor, driving = pair_terms(p)
+        amplitudes = out_ref[p]
+        residual = driving + esum * amplitudes + total
+        amplitudes = amplitudes - residual / divisor
+        out_ref[p] = amplitudes
+        if r < ITERS:
+            rounds[r + 1][me, p] = amplitudes.astype(jnp.bfloat16)
+
+    start_own(0)
+    start_own(1)
+    run(0, [ladder_piece(1, p, True) for p in range(own_pairs)])
+    for r in range(1, ITERS + 1):
+        if r == 1:
+            run(r, [margin_piece(p) for p in range(own_pairs)])
+            finish_sends(0)
+        else:
+            run(r, [ladder_piece(r, p, False) for p in range(own_pairs)])
+        finish_sends(r)
+        for p in range(own_pairs):
+            couple(r, p)
+        if r < ITERS:
+            start_own(r + 1)
+
+
+def fused(
+    n, pno_basis, pno_count, partner_owner, partner_local, exchange_k, ladder_factor,
+    pno_energy, occ_energy, coupling_fock,
+):
+    own_pairs, domain, orbitals = pno_basis.shape
+    fitted = ladder_factor.shape[1]
+    partners = partner_owner.shape[1]
+    smem = pl.BlockSpec(memory_space=pltpu.SMEM)
+    vmem = pl.BlockSpec(memory_space=pltpu.VMEM)
+    depth = n // 8
+    amps = pltpu.VMEM((n, own_pairs, orbitals, orbitals), jnp.bfloat16)
+    return pl.pallas_call(
+        functools.partial(kernel, n),
+        out_shape=jax.ShapeDtypeStruct((own_pairs, orbitals, orbitals), jnp.float32),
+        in_specs=[vmem, smem, smem, smem, vmem, pl.BlockSpec(memory_space=pl.ANY), vmem, vmem, smem, smem],
+        out_specs=vmem,
+        scratch_shapes=[
+            pltpu.VMEM((n, own_pairs, domain, orbitals), jnp.bfloat16),
+            amps,
+            amps,
+            pltpu.VMEM(ladder_factor.shape, jnp.bfloat16),
+            pltpu.VMEM((own_pairs, orbitals, partners * orbitals), jnp.bfloat16),
+            pltpu.VMEM((own_pairs, orbitals, orbitals), jnp.float32),
+            pltpu.SemaphoreType.DMA((own_pairs,)),
+            pltpu.SemaphoreType.DMA((ITERS + 1, 2, n // 2)),
+            pltpu.SemaphoreType.DMA((ITERS + 1, 2)),
+            pltpu.SemaphoreType.DMA((2, 2, 2, n // 2)),
+            pltpu.SemaphoreType.DMA((2, 2, 2)),
+            pltpu.SemaphoreType.DMA((2, 2)),
+        ],
+        compiler_params=pltpu.CompilerParams(
+            collective_id=0, has_side_effects=True, vmem_limit_bytes=VMEM_BYTES
+        ),
+        name="jacobi",
+    )(
+        pno_basis, pno_count, partner_owner, partner_local, exchange_k, ladder_factor,
+        pno_energy, pno_energy.T, occ_energy, coupling_fock.astype(jnp.float32),
+    )
+
+
+def shards(*args):
+    n = lax.axis_size("pairs")
+    own_pairs, domain, orbitals = args[0].shape
+    gathered = n * own_pairs * orbitals * (domain + 2 * orbitals) * 2
+    resident = args[5].size * 2 + own_pairs * orbitals * orbitals * (2 * args[2].shape[1] + 16)
+    fits = gathered + resident < VMEM_BYTES - (4 << 20)
+    if n % 16 == 0 and own_pairs % 4 == 0 and args[2].shape[1] % 2 == 0 and fits:
+        return fused(n, *args)
+    return gathered_rows(*args)
+
+
+def gathered_rows(
     pno_basis,
     pno_count,
     partner_owner,

time: 394 us -> 233 us (0.59)
  waiting for transfers between devices: 261 us -> 0 us
  Pallas kernels: 0 us -> 228 us
  matrix products: 79.9 us -> 0 us
  local copies, waits for them, and re-layouts: 24 us -> 3.29 us
  between operations: 13.2 us -> 0.01 us
  other arithmetic: 14.1 us -> 1.27 us
    all_gather x4 -> x0, waiting for transfers between devices: 261 us -> none  [the longest x3 169 us: shards(): every_amps = lax.all_gather(sent_amps, 'pairs', axis=0, tiled=True)]
    pallas_call x0 -> x1, Pallas kernels: none -> 228 us  [fused(): pl.pallas_call(functools.partial(kernel, n), out_shape=jax.ShapeDtypeStru...]
    dot_general x19 -> x0, matrix products: 79.9 us -> none  [the longest x15 56.1 us: add_group(): jnp.einsum('rqad,rqbd->rab', ladder_half, factors, preferred_element_type...]
    gather x4 -> x0, local copies, waits for them, and re-layouts: 21.6 us -> none  [the longest x3 13.6 us: shards(): partner_amps = every_amps[partner]]
    convert_element_type x5 -> x1, other arithmetic: 9.07 us -> 1.27 us  [fused(): coupling_fock.astype(jnp.float32)]
  transfers between devices with their start and end apart: 4 -> 0, of which waited for: 4 -> 0; matrix products, arithmetic and copies ran while one was open for 16% -> 0% of each run, Pallas kernels for 0% -> 0%
where the time goes in v2:
time: 233 us
  Pallas kernels  228 us (98%)
  local copies, waits for them, and re-layouts  3.29 us (1%)
    pallas_call x1, Pallas kernels, fused(): pl.pallas_call(functools.partial(kernel, n), out_shape=jax.ShapeDtypeStru...  228 us

profile of v2, /device:TPU:0, one launch (start us, length us, event | category | flops | bytes accessed | tf_op | source)
XLA Modules:
  0.0 232.9 jit_solution(10486020552962106360)
XLA Ops:
  0.0 1.3 convert_element_type.3.fock_ref
  1.3 1.4 copy.10
  2.7 228.3 %jacobi.1 = f32[8,128,128]{2,1,0:T(8,128)} custom-call(bf16[8,192,128]{2,1,0:T(8,128)(2,1)} %basis_ref.1, s32[8]{0:T(128)} %count_ref.1, s32[8,12]{1,0:T(8,128)} %owner_ref.1, s32[8,12]{1,0:T(8,128)} %local_ref.1, bf16[8,128,128]{2,1,0:T(8,128)(2,1)} %exchange_ref.1, bf16[8,40,128,128]{3,2,1,0:T(8,128)(2,1)} %ladder_hbm.1, f32[8,128]{1,0:T(8,128)} %energy_ref.1, ...), custom_call_target="tpu_custom_call" | custom-call | tf_op jit(solution)/shard_map/jacobi/pallas_call | solution.py:292
  231.0 1.9 copy.12

commit v3 on v2

--- a/solution.py
+++ b/solution.py
@@ -41,7 +41,9 @@
     sibling = me + 1 - 2 * core
     bases = (me, near_dev, far_dev, me + shift_near + shift_far)
     tail = own_pairs // 4
-    spans = ((0, own_pairs - tail), (own_pairs - tail, tail))
+    half = (own_pairs - tail) // 2
+    spans = ((0, half), (half, own_pairs - tail - half), (own_pairs - tail, tail))
+    kinds = (0, 0, 1)
     rounds = (all_basis, amps_a, amps_b, amps_a)
 
     loads = [
@@ -73,7 +75,7 @@
         remote(r, t, owner, sibling, send_sib.at[r % 2, t], recv_sib.at[r, t]).start()
 
     def forward(r, t, owner, via, up=None):
-        if t == 0:
+        if kinds[t] == 0:
             if via in ("own", "line"):
                 if up is None or up is False:
                     send_line(r, t, owner, False)
@@ -98,7 +100,7 @@
         forward(r, t, owner, via, up)
 
     def start_own(r):
-        for t in (0, 1):
+        for t in reversed(range(len(spans))):
             forward(r, t, me, "own")
 
     vias = ("own", "near", "far", "far")
@@ -115,24 +117,23 @@
                     owner = bases[b] + stride * (k if up is False else -k)
 
                     def inner():
-                        if t == 0:
-                            arrive(r, 0, owner, "line" if b == 0 else vias[b], up if b == 0 else None)
+                        if kinds[t] == 0:
+                            arrive(r, t, owner, "line" if b == 0 else vias[b], up if b == 0 else None)
                         else:
-                            arrive(r, 1, owner, "line", up)
+                            arrive(r, t, owner, "line", up)
                     pl.when((place >= 0) & (place < depth))(inner)
             found.append(go)
 
-        for k in range(depth):
-            for b in range(4):
-                if k == 0:
-                    if b == 0:
-                        continue
-                    at(1, b, 0, None)
-                    at(0, b, 0, None)
-                else:
-                    for t in (0, 1):
-                        for up in (True, False):
-                            at(t, b, k, up)
+        order = [(1, 1, 0), (0, 0, 1), (1, 2, 0), (0, 1, 0), (1, 3, 0), (1, 0, 1), (0, 0, 2), (0, 1, 1), (1, 1, 1), (1, 2, 1), (0, 0, 3), (1, 3, 1), (0, 1, 2)]
+        order += [(1, 0, 2), (0, 2, 0), (1, 1, 2), (0, 3, 0), (0, 1, 3), (1, 2, 2), (0, 2, 1), (1, 3, 2), (0, 3, 1), (0, 2, 2), (1, 0, 3), (0, 3, 2), (1, 1, 3)]
+        order = [event for event in order if event[2] < depth]
+        every = [(t, b, k) for k in range(depth) for t in (0, 1) for b in (2, 3, 0, 1)]
+        order += [event for event in every if event not in order and event != (0, 0, 0) and event != (1, 0, 0)]
+        for kind, b, k in order:
+            for t in range(len(spans)):
+                for up in (None,) if k == 0 else (True, False):
+                    if kinds[t] == kind:
+                        at(t, b, k, up)
         return found
 
     def run(r, pieces):
@@ -144,8 +145,8 @@
             for piece in pieces[done:upto]:
                 piece()
             done = upto
-        whole(r, 0, n // 2, recv_sib.at[r, 0])
-        whole(r, 1, n // 2, recv_sib.at[r, 1])
+        for t in range(len(spans)):
+            whole(r, t, n // 2, recv_sib.at[r, t])
 
     def whole(r, t, number, sem):
         lo, cnt = spans[t]
@@ -153,11 +154,11 @@
         pltpu.make_async_copy(view, view, sem).wait()
 
     def finish_sends(r):
-        for t in (0, 1):
-            whole(r, t, depth if t == 0 else 1, send_near.at[r % 2, t, 0])
-            whole(r, t, 2 * depth if t == 0 else 2, send_near.at[r % 2, t, 1])
+        for t in range(len(spans)):
+            whole(r, t, depth if kinds[t] == 0 else 1, send_near.at[r % 2, t, 0])
+            whole(r, t, 2 * depth if kinds[t] == 0 else 2, send_near.at[r % 2, t, 1])
             whole(r, t, n // 2, send_sib.at[r % 2, t])
-            for b in range(1 if t == 0 else 4):
+            for b in range(1 if kinds[t] == 0 else 4):
                 for up in (True, False):
                     for j in range(depth):
                         owner = bases[b] + stride * (j - line)
@@ -268,14 +269,17 @@
     for r in range(1, ITERS + 1):
         if r == 1:
             run(r, [margin_piece(p) for p in range(own_pairs)])
-            finish_sends(0)
         else:
             run(r, [ladder_piece(r, p, False) for p in range(own_pairs)])
-        finish_sends(r)
-        for p in range(own_pairs):
-            couple(r, p)
-        if r < ITERS:
-            start_own(r + 1)
+        if r == 1:
+            finish_sends(0)
+        for t in reversed(range(len(spans))):
+            for p in range(spans[t][0], spans[t][0] + spans[t][1]):
+                couple(r, p)
+            if t == 0:
+                finish_sends(r)
+            if r < ITERS:
+                forward(r + 1, t, me, "own")
 
 
 def fused(
@@ -302,11 +306,11 @@
             pltpu.VMEM((own_pairs, orbitals, partners * orbitals), jnp.bfloat16),
             pltpu.VMEM((own_pairs, orbitals, orbitals), jnp.float32),
             pltpu.SemaphoreType.DMA((own_pairs,)),
-            pltpu.SemaphoreType.DMA((ITERS + 1, 2, n // 2)),
-            pltpu.SemaphoreType.DMA((ITERS + 1, 2)),
-            pltpu.SemaphoreType.DMA((2, 2, 2, n // 2)),
-            pltpu.SemaphoreType.DMA((2, 2, 2)),
-            pltpu.SemaphoreType.DMA((2, 2)),
+            pltpu.SemaphoreType.DMA((ITERS + 1, 3, n // 2)),
+            pltpu.SemaphoreType.DMA((ITERS + 1, 3)),
+            pltpu.SemaphoreType.DMA((2, 2, 3, n // 2)),
+            pltpu.SemaphoreType.DMA((2, 3, 2)),
+            pltpu.SemaphoreType.DMA((2, 3)),
         ],
         compiler_params=pltpu.CompilerParams(
             collective_id=0, has_side_effects=True, vmem_limit_bytes=VMEM_BYTES

time: 233 us -> 167 us (0.72)
  Pallas kernels: 228 us -> 162 us
    pallas_call x1, Pallas kernels: 228 us -> 162 us  [fused(): pl.pallas_call(functools.partial(kernel, n), out_shape=jax.ShapeDtypeStru...]
where the time goes in v3:
time: 167 us
  Pallas kernels  162 us (97%)
  local copies, waits for them, and re-layouts  3.29 us (2%)
    pallas_call x1, Pallas kernels, fused(): pl.pallas_call(functools.partial(kernel, n), out_shape=jax.ShapeDtypeStru...  162 us

profile of v3, /device:TPU:0, one launch (start us, length us, event | category | flops | bytes accessed | tf_op | source)
XLA Modules:
  0.0 166.5 jit_solution(18391292283462319758)
XLA Ops:
  0.0 1.3 convert_element_type.3.fock_ref
  1.3 1.4 copy.10
  2.7 162.0 %jacobi.1 = f32[8,128,128]{2,1,0:T(8,128)} custom-call(bf16[8,192,128]{2,1,0:T(8,128)(2,1)} %basis_ref.1, s32[8]{0:T(128)} %count_ref.1, s32[8,12]{1,0:T(8,128)} %owner_ref.1, s32[8,12]{1,0:T(8,128)} %local_ref.1, bf16[8,128,128]{2,1,0:T(8,128)(2,1)} %exchange_ref.1, bf16[8,40,128,128]{3,2,1,0:T(8,128)(2,1)} %ladder_hbm.1, f32[8,128]{1,0:T(8,128)} %energy_ref.1, ...), custom_call_target="tpu_custom_call" | custom-call | tf_op jit(solution)/shard_map/jacobi/pallas_call | solution.py:296
  164.7 1.9 %copy.12 = f32[8,128,128]{2,1,0:T(8,128)} copy(f32[8,128,128]{2,1,0:T(8,128)} %jacobi.1) | data formatting | bytes 1048576
